TPU v7x, 512 devices: a whole 4x4x16 slice. The times are simulated.
512 devices in a mesh: island: 16 (over z), fsdp: 32 (over x, y, core).
Axes of the slice: x: 4, y: 4, z: 16, core: 2. Of those that a mesh axis runs over, the one named last changes fastest.
Arguments:
- activations: bfloat16 [16, 11776, 4096], P('island', 'fsdp'), may hold values from -6 to 6
- key_grad: bfloat16 [16, 11776, 512], P('island', 'fsdp'), may hold values from -0.0546875 to 0.0546875
- island_weight: float32 [16, 4096, 512], P('island', 'fsdp'), may hold values from -0.09375 to 0.09375
- adam_m: float32 [16, 4096, 512], P('island', 'fsdp'), may hold values from -6 to 6
- adam_v: float32 [16, 4096, 512], P('island', 'fsdp'), may hold values from 0.2 to 2
- anchor: float32 [16, 256, 512], P('island', 'fsdp'), may hold values from -0.09375 to 0.09375
- outer_momentum: float32 [16, 256, 512], P('island', 'fsdp'), may hold values from -0.09375 to 0.09375
Outputs:
- adam_m_next: float32 [16, 4096, 512], P('island', 'fsdp')
- adam_v_next: float32 [16, 4096, 512], P('island', 'fsdp')
- island_weight_next: float32 [4096, 512], P('fsdp')
- anchor_next: float32 [16, 256, 512], P('island', 'fsdp')
- momentum_next: float32 [16, 256, 512], P('island', 'fsdp')
All inputs are finite; a program needn't handle non-finite values.
Results may differ from a plain program's by a relative error of at most 0.0003.
Values may be sent and summed in bfloat16 or wider, within the bound.
A program may use at most 64 MiB of HBM per device.

v0:
```python
import jax
import jax.numpy as jnp
from jax import lax
from jax.sharding import PartitionSpec as P

beta_first = 0.9
beta_second = 0.95
epsilon = 1e-08
inner_rate = 0.0004
decay_rate = 0.1
outer_beta = 0.9
outer_rate = 0.7


def swapped(value, axis, bit):
    return lax.ppermute(value, axis, [(i, i ^ 1 << bit) for i in range(lax.axis_size(axis))])


def shards(activations, key_grad, island_weight, adam_m, adam_v, anchor, outer_momentum):
    inputs = activations[0]
    tangent = key_grad[0]
    row_count = island_weight.shape[1]
    columns = lax.all_to_all(inputs, "fsdp", split_axis=1, concat_axis=0, tiled=True)
    grad = lax.dot_general(
        columns,
        lax.all_gather(tangent, "fsdp", axis=0, tiled=True),
        (((0,), (0,)), ((), ())),
        preferred_element_type=jnp.float32,
    )
    m_next = beta_first * adam_m[0] + (1.0 - beta_first) * grad
    v_next = beta_second * adam_v[0] + (1.0 - beta_second) * grad * grad
    weight = island_weight[0]
    stepped = weight - inner_rate * (m_next / (jnp.sqrt(v_next) + epsilon) + decay_rate * weight)
    islands = lax.axis_size("island")
    levels = islands.bit_length() - 1
    share_rows = row_count // islands
    position = lax.axis_index("island")
    summed = stepped
    for bit in range(levels):
        summed = summed + swapped(summed, "island", bit)
    own_sum = lax.dynamic_slice_in_dim(summed, position * share_rows, share_rows, 0)
    anchor_block = anchor[0]
    shift = anchor_block - own_sum / float(islands)
    moment = outer_beta * outer_momentum[0] + shift
    new_anchor = anchor_block - outer_rate * (shift + outer_beta * moment)
    refreshed = lax.all_gather(new_anchor, "island", axis=0, tiled=True)
    return (m_next[None], v_next[None], refreshed, new_anchor[None], moment[None])


def solution(mesh):
    return jax.shard_map(
        shards,
        mesh=mesh,
        in_specs=(
            P("island", "fsdp", None),
            P("island", "fsdp", None),
            P("island", "fsdp", None),
            P("island", "fsdp", None),
            P("island", "fsdp", None),
            P("island", "fsdp", None),
            P("island", "fsdp", None),
        ),
        out_specs=(
            P("island", "fsdp", None),
            P("island", "fsdp", None),
            P("fsdp", None),
            P("island", "fsdp", None),
            P("island", "fsdp", None),
        ),
        check_vma=False,
    )
```

profile of v0, /device:TPU:2, one launch (start us, length us, event | category | flops | bytes accessed | tf_op | source)
XLA Modules:
  0.0 242.4 jit_solution(13812907711596420552)
XLA Ops:
  7.2 0.0 all-gather.3.cloned.1.call-start
  7.2 0.7 all-gather.3.cloned.1.call-update
  7.9 2.6 %copy.14 = bf16[46,8,32,128]{3,2,1,0:T(8,128)(2,1)S(1)} copy(bf16[46,8,32,128]{3,1,2,0:T(8,128)(2,1)} %bitcast.55) | data formatting | bytes 6029312
  10.5 1.2 copy.13
  11.7 0.0 copy-start
  11.7 0.0 copy-start.1
  11.7 50.5 %all_to_all.19 = bf16[368,32,128]{2,0,1:T(8,128)(2,1)S(1)} all-to-all(bf16[368,32,128]{2,0,1:T(8,128)(2,1)S(1)} %copy.13), channel_id=1, replica_groups=mesh['island'=16,'fsdp'=32] {'fsdp'}, dimensions={1} | all-to-all | bytes 6029312 | tf_op jit(solution)/shard_map/all_to_all | solution.py:23
  62.3 47.1 %all-gather.3.cloned.1.call-done = bf16[1,11776,512]{2,1,0:T(8,128)(2,1)} async-done(((bf16[1,368,512]{2,1,0:T(8,128)(2,1)}), bf16[1,11776,512]{2,1,0:T(8,128)(2,1)}) %all-gather.3.cloned.1.call-update) | async-done | bytes 12058640 | tf_op jit(solution)/shard_map/all_gather | solution.py:26
  109.4 0.0 copy-done
  109.4 0.0 copy-done.1
  109.4 0.0 copy-start.3
  109.4 7.1 %bitcast_subtract_fusion = (f32[128,512]{1,0:T(8,128)S(1)}, f32[1,128,512]{2,1,0:T(8,128)}, f32[1,128,512]{2,1,0:T(8,128)}) fusion(f32[1,128,512]{2,1,0:T(8,128)S(1)} %copy-done, f32[1,128,512]{2,1,0:T(8,128)S(1)} %copy-done.1, f32[1,128,512]{2,1,0:T(8,128)} %param.11, bf16[11776,128]{1,0:T(8,128)(2,1)S(1)} %bitcast.53, ...), kind=kOutput, calls=%fused_computation.4 | convolution fusion | flops 1544355840 | bytes 16646144 | tf_op jit(solution)/shard_map/dot_general | solution.py:24
  116.5 3.4 %collective-permute-start = (f32[128,512]{1,0:T(8,128)S(1)}, f32[128,512]{1,0:T(8,128)S(1)}, u32[]{:S(2)}, u32[]{:S(2)}) collective-permute-start(f32[128,512]{1,0:T(8,128)S(1)} %get-tuple-element.7), channel_id=1, source_target_pairs={{0,32},{32,0},{64,96},{96,64},{128,160},{160,128},{192,224},{224,1... | collective-permute-start | bytes 786440 | tf_op jit(solution)/shard_map/ppermute | solution.py:16
  120.0 6.9 %collective-permute-done = f32[128,512]{1,0:T(8,128)S(1)} collective-permute-done((f32[128,512]{1,0:T(8,128)S(1)}, f32[128,512]{1,0:T(8,128)S(1)}, u32[]{:S(2)}, u32[]{:S(2)}) %collective-permute-start) | collective-permute-done | bytes 262176 | tf_op jit(solution)/shard_map/ppermute | solution.py:16
  126.9 4.5 %collective-permute-start.1 = (f32[128,512]{1,0:T(8,128)S(1)}, f32[128,512]{1,0:T(8,128)S(1)}, u32[]{:S(2)}, u32[]{:S(2)}) collective-permute-start(f32[128,512]{1,0:T(8,128)S(1)} %add.41), channel_id=1, source_target_pairs={{0,64},{32,96},{64,0},{96,32},{128,192},{160,224},{192,128},{224,1... | collective-permute-start | bytes 786440 | tf_op jit(solution)/shard_map/ppermute | solution.py:16
  131.4 11.6 %collective-permute-done.1 = f32[128,512]{1,0:T(8,128)S(1)} collective-permute-done((f32[128,512]{1,0:T(8,128)S(1)}, f32[128,512]{1,0:T(8,128)S(1)}, u32[]{:S(2)}, u32[]{:S(2)}) %collective-permute-start.1) | collective-permute-done | bytes 262176 | tf_op jit(solution)/shard_map/ppermute | solution.py:16
  143.0 7.6 %collective-permute-start.2 = (f32[128,512]{1,0:T(8,128)S(1)}, f32[128,512]{1,0:T(8,128)S(1)}, u32[]{:S(2)}, u32[]{:S(2)}) collective-permute-start(f32[128,512]{1,0:T(8,128)S(1)} %add.42), channel_id=1, source_target_pairs={{0,128},{32,160},{64,192},{96,224},{128,0},{160,32},{192,64},{224,... | collective-permute-start | bytes 786440 | tf_op jit(solution)/shard_map/ppermute | solution.py:16
  150.7 21.2 %collective-permute-done.2 = f32[128,512]{1,0:T(8,128)S(1)} collective-permute-done((f32[128,512]{1,0:T(8,128)S(1)}, f32[128,512]{1,0:T(8,128)S(1)}, u32[]{:S(2)}, u32[]{:S(2)}) %collective-permute-start.2) | collective-permute-done | bytes 262176 | tf_op jit(solution)/shard_map/ppermute | solution.py:16
  171.9 11.5 %collective-permute-start.3 = (f32[128,512]{1,0:T(8,128)S(1)}, f32[128,512]{1,0:T(8,128)S(1)}, u32[]{:S(2)}, u32[]{:S(2)}) collective-permute-start(f32[128,512]{1,0:T(8,128)S(1)} %add.43), channel_id=1, source_target_pairs={{0,256},{32,288},{64,320},{96,352},{128,384},{160,416},{192,448},{... | collective-permute-start | bytes 786440 | tf_op jit(solution)/shard_map/ppermute | solution.py:16
  183.4 22.2 %collective-permute-done.3 = f32[128,512]{1,0:T(8,128)S(1)} collective-permute-done((f32[128,512]{1,0:T(8,128)S(1)}, f32[128,512]{1,0:T(8,128)S(1)}, u32[]{:S(2)}, u32[]{:S(2)}) %collective-permute-start.3) | collective-permute-done | bytes 262176 | tf_op jit(solution)/shard_map/ppermute | solution.py:16
  205.6 0.0 copy-done.3
  205.6 1.3 fusion.9
  207.0 0.0 copy-start.2
  207.0 27.9 %all_gather.7 = f32[128,512]{1,0:T(8,128)S(1)} all-gather(f32[8,512]{1,0:T(8,128)S(1)} %get-tuple-element.6), channel_id=1, replica_groups=mesh['island'=16,'fsdp'=32] {'island'}, dimensions={0}, use_global_device_ids=true | all-gather | bytes 278528 | tf_op jit(solution)/shard_map/all_gather | solution.py:46
  234.9 0.7 copy.16
  235.6 0.0 copy-done.2
  (3 shorter events, 0.1 us)
Async XLA Ops:
  7.2 102.2 %all-gather.3.cloned.1.call-start = ((), (), s32[]{:S(2)}) async-start(), calls=%async_computation.1 | async-start | bytes 12435456 | tf_op jit(solution)/shard_map/all_gather | solution.py:26
  11.7 97.6 %copy-start = (f32[1,128,512]{2,1,0:T(8,128)S(1)}, f32[1,128,512]{2,1,0:T(8,128)}, u32[]{:S(2)}) copy-start(f32[1,128,512]{2,1,0:T(8,128)} %param.9) | copy-start | bytes 786436
  11.7 97.6 %copy-start.1 = (f32[1,128,512]{2,1,0:T(8,128)S(1)}, f32[1,128,512]{2,1,0:T(8,128)}, u32[]{:S(2)}) copy-start(f32[1,128,512]{2,1,0:T(8,128)} %param.10) | copy-start | bytes 786436
  109.4 96.3 %copy-start.3 = (f32[1,8,512]{2,1,0:T(8,128)S(1)}, f32[1,8,512]{2,1,0:T(8,128)}, u32[]{:S(2)}) copy-start(f32[1,8,512]{2,1,0:T(8,128)} %param.13) | copy-start | bytes 49156
  116.5 10.3 %collective-permute-start = (f32[128,512]{1,0:T(8,128)S(1)}, f32[128,512]{1,0:T(8,128)S(1)}, u32[]{:S(2)}, u32[]{:S(2)}) collective-permute-start(f32[128,512]{1,0:T(8,128)S(1)} %get-tuple-element.7), channel_id=1, source_target_pairs={{0,32},{32,0},{64,96},{96,64},{128,160},{160,128},{192,224},{224,1... | collective-permute-start | bytes 786440 | tf_op jit(solution)/shard_map/ppermute | solution.py:16
  126.9 16.1 %collective-permute-start.1 = (f32[128,512]{1,0:T(8,128)S(1)}, f32[128,512]{1,0:T(8,128)S(1)}, u32[]{:S(2)}, u32[]{:S(2)}) collective-permute-start(f32[128,512]{1,0:T(8,128)S(1)} %add.41), channel_id=1, source_target_pairs={{0,64},{32,96},{64,0},{96,32},{128,192},{160,224},{192,128},{224,1... | collective-permute-start | bytes 786440 | tf_op jit(solution)/shard_map/ppermute | solution.py:16
  143.0 28.9 %collective-permute-start.2 = (f32[128,512]{1,0:T(8,128)S(1)}, f32[128,512]{1,0:T(8,128)S(1)}, u32[]{:S(2)}, u32[]{:S(2)}) collective-permute-start(f32[128,512]{1,0:T(8,128)S(1)} %add.42), channel_id=1, source_target_pairs={{0,128},{32,160},{64,192},{96,224},{128,0},{160,32},{192,64},{224,... | collective-permute-start | bytes 786440 | tf_op jit(solution)/shard_map/ppermute | solution.py:16
  171.9 33.7 %collective-permute-start.3 = (f32[128,512]{1,0:T(8,128)S(1)}, f32[128,512]{1,0:T(8,128)S(1)}, u32[]{:S(2)}, u32[]{:S(2)}) collective-permute-start(f32[128,512]{1,0:T(8,128)S(1)} %add.43), channel_id=1, source_target_pairs={{0,256},{32,288},{64,320},{96,352},{128,384},{160,416},{192,448},{... | collective-permute-start | bytes 786440 | tf_op jit(solution)/shard_map/ppermute | solution.py:16
  207.0 28.6 %copy-start.2 = (f32[8,512]{1,0:T(8,128)}, f32[8,512]{1,0:T(8,128)S(1)}, u32[]{:S(2)}) copy-start(f32[8,512]{1,0:T(8,128)S(1)} %get-tuple-element.6) | copy-start | bytes 49156
Sparse Core Ops, SparseCore 0:
  11.1 98.1 all-gather.2
where the time goes:
time: 243 us; the launch traced here: 242 us
  waiting for transfers between devices  110 us (45%)
  blocking collectives  78.4 us (32%)
  starting transfers between devices  27.1 us (11%)
  between operations  14.1 us (6%)
  matrix products  7.15 us (3%)
  local copies, waits for them, and re-layouts  4.52 us (2%)
    ppermute x4, waiting for transfers between devices, swapped(): lax.ppermute(value, axis, [(i, i ^ 1 << bit) for i in range(lax.axis_size...  61.9 us
    all_to_all x1, blocking collectives, shards(): lax.all_to_all(inputs, 'fsdp', split_axis=1, concat_axis=0, tiled=True)  50.5 us
    all_gather x1, waiting for transfers between devices, shards(): lax.all_gather(tangent, 'fsdp', axis=0, tiled=True)  47.1 us
    all_gather x1, blocking collectives, shards(): refreshed = lax.all_gather(new_anchor, 'island', axis=0, tiled=True)  27.9 us
    ppermute x4, starting transfers between devices, swapped(): lax.ppermute(value, axis, [(i, i ^ 1 << bit) for i in range(lax.axis_size...  27.1 us
    dot_general x1, matrix products, shards(): lax.dot_general(columns, lax.all_gather(tangent, 'fsdp', axis=0, tiled=Tr...  7.15 us
  transfers between devices with their start and end apart: 5, of which 5 were waited for; matrix products, arithmetic and copies ran while one was open for 2% of the time, Pallas kernels for 0%

commit v1 on v0

--- a/solution.py
+++ b/solution.py
@@ -43,7 +43,8 @@
     shift = anchor_block - own_sum / float(islands)
     moment = outer_beta * outer_momentum[0] + shift
     new_anchor = anchor_block - outer_rate * (shift + outer_beta * moment)
-    refreshed = lax.all_gather(new_anchor, "island", axis=0, tiled=True)
+    prior = jnp.concatenate([new_anchor] * lax.axis_size("island"), 0)
+    refreshed = lax.all_to_all(prior, "island", 0, 0, tiled=True)
     return (m_next[None], v_next[None], refreshed, new_anchor[None], moment[None])
 
 

time: 243 us -> 238 us (0.979)
  blocking collectives: 78.4 us -> 73.5 us
    all_gather x1 -> x0, blocking collectives: 27.9 us -> none  [shards(): refreshed = lax.all_gather(new_anchor, 'island', axis=0, tiled=True)]
    all_to_all x0 -> x1, blocking collectives: none -> 22.9 us  [shards(): refreshed = lax.all_to_all(prior, 'island', 0, 0, tiled=True)]
where the time goes in v1:
time: 238 us; the launch traced here: 237 us
  waiting for transfers between devices  109 us (46%)
  blocking collectives  73.5 us (31%)
  starting transfers between devices  27.1 us (11%)
  between operations  14.2 us (6%)
  matrix products  7.15 us (3%)
  local copies, waits for them, and re-layouts  4.57 us (2%)
    ppermute x4, waiting for transfers between devices, swapped(): lax.ppermute(value, axis, [(i, i ^ 1 << bit) for i in range(lax.axis_size...  61.6 us
    all_to_all x1, blocking collectives, shards(): lax.all_to_all(inputs, 'fsdp', split_axis=1, concat_axis=0, tiled=True)  50.5 us
    all_gather x1, waiting for transfers between devices, shards(): lax.all_gather(tangent, 'fsdp', axis=0, tiled=True)  47.1 us
    ppermute x4, starting transfers between devices, swapped(): lax.ppermute(value, axis, [(i, i ^ 1 << bit) for i in range(lax.axis_size...  27.1 us
    all_to_all x1, blocking collectives, shards(): refreshed = lax.all_to_all(prior, 'island', 0, 0, tiled=True)  22.9 us
    dot_general x1, matrix products, shards(): lax.dot_general(columns, lax.all_gather(tangent, 'fsdp', axis=0, tiled=Tr...  7.15 us
  transfers between devices with their start and end apart: 5, of which 5 were waited for; matrix products, arithmetic and copies ran while one was open for 2% of the time, Pallas kernels for 0%

profile of v1, /device:TPU:2, one launch (start us, length us, event | category | flops | bytes accessed | tf_op | source)
XLA Modules:
  0.0 237.4 jit_solution(18385744522132543502)
XLA Ops:
  7.2 0.0 all-gather.3.cloned.1.call-start
  7.2 0.7 all-gather.3.cloned.1.call-update
  7.9 2.6 %copy.14 = bf16[46,8,32,128]{3,2,1,0:T(8,128)(2,1)S(1)} copy(bf16[46,8,32,128]{3,1,2,0:T(8,128)(2,1)} %bitcast.60) | data formatting | bytes 6029312
  10.5 1.2 copy.13
  11.7 0.0 copy-start.1
  11.7 0.0 copy-start.2
  11.7 50.5 %all_to_all.31 = bf16[368,32,128]{2,0,1:T(8,128)(2,1)S(1)} all-to-all(bf16[368,32,128]{2,0,1:T(8,128)(2,1)S(1)} %copy.13), channel_id=1, replica_groups=mesh['island'=16,'fsdp'=32] {'fsdp'}, dimensions={1} | all-to-all | bytes 6029312 | tf_op jit(solution)/shard_map/all_to_all | solution.py:23
  62.3 47.1 %all-gather.3.cloned.1.call-done = bf16[1,11776,512]{2,1,0:T(8,128)(2,1)} async-done(((bf16[1,368,512]{2,1,0:T(8,128)(2,1)}), bf16[1,11776,512]{2,1,0:T(8,128)(2,1)}) %all-gather.3.cloned.1.call-update) | async-done | bytes 12058640 | tf_op jit(solution)/shard_map/all_gather | solution.py:26
  109.4 0.0 copy-done.1
  109.4 0.0 copy-done.2
  109.4 0.0 copy-start.3
  109.4 7.1 %bitcast_subtract_fusion = (f32[128,512]{1,0:T(8,128)S(1)}, f32[1,128,512]{2,1,0:T(8,128)}, f32[1,128,512]{2,1,0:T(8,128)}) fusion(f32[1,128,512]{2,1,0:T(8,128)S(1)} %copy-done.1, f32[1,128,512]{2,1,0:T(8,128)S(1)} %copy-done.2, f32[1,128,512]{2,1,0:T(8,128)} %param.11, bf16[11776,128]{1,0:T(8,128)(2,1)S(1)} %bitcast.57, ...), kind=kOutput, calls=%fused_computation.4 | convolution fusion | flops 1544355840 | bytes 16646144 | tf_op jit(solution)/shard_map/dot_general | solution.py:24
  116.5 3.4 %collective-permute-start = (f32[128,512]{1,0:T(8,128)S(1)}, f32[128,512]{1,0:T(8,128)S(1)}, u32[]{:S(2)}, u32[]{:S(2)}) collective-permute-start(f32[128,512]{1,0:T(8,128)S(1)} %get-tuple-element.8), channel_id=1, source_target_pairs={{0,32},{32,0},{64,96},{96,64},{128,160},{160,128},{192,224},{224,1... | collective-permute-start | bytes 786440 | tf_op jit(solution)/shard_map/ppermute | solution.py:16
  120.0 6.9 %collective-permute-done = f32[128,512]{1,0:T(8,128)S(1)} collective-permute-done((f32[128,512]{1,0:T(8,128)S(1)}, f32[128,512]{1,0:T(8,128)S(1)}, u32[]{:S(2)}, u32[]{:S(2)}) %collective-permute-start) | collective-permute-done | bytes 262176 | tf_op jit(solution)/shard_map/ppermute | solution.py:16
  126.9 4.5 %collective-permute-start.1 = (f32[128,512]{1,0:T(8,128)S(1)}, f32[128,512]{1,0:T(8,128)S(1)}, u32[]{:S(2)}, u32[]{:S(2)}) collective-permute-start(f32[128,512]{1,0:T(8,128)S(1)} %add.41), channel_id=1, source_target_pairs={{0,64},{32,96},{64,0},{96,32},{128,192},{160,224},{192,128},{224,1... | collective-permute-start | bytes 786440 | tf_op jit(solution)/shard_map/ppermute | solution.py:16
  131.4 11.6 %collective-permute-done.1 = f32[128,512]{1,0:T(8,128)S(1)} collective-permute-done((f32[128,512]{1,0:T(8,128)S(1)}, f32[128,512]{1,0:T(8,128)S(1)}, u32[]{:S(2)}, u32[]{:S(2)}) %collective-permute-start.1) | collective-permute-done | bytes 262176 | tf_op jit(solution)/shard_map/ppermute | solution.py:16
  143.0 7.6 %collective-permute-start.2 = (f32[128,512]{1,0:T(8,128)S(1)}, f32[128,512]{1,0:T(8,128)S(1)}, u32[]{:S(2)}, u32[]{:S(2)}) collective-permute-start(f32[128,512]{1,0:T(8,128)S(1)} %add.42), channel_id=1, source_target_pairs={{0,128},{32,160},{64,192},{96,224},{128,0},{160,32},{192,64},{224,... | collective-permute-start | bytes 786440 | tf_op jit(solution)/shard_map/ppermute | solution.py:16
  150.7 21.2 %collective-permute-done.2 = f32[128,512]{1,0:T(8,128)S(1)} collective-permute-done((f32[128,512]{1,0:T(8,128)S(1)}, f32[128,512]{1,0:T(8,128)S(1)}, u32[]{:S(2)}, u32[]{:S(2)}) %collective-permute-start.2) | collective-permute-done | bytes 262176 | tf_op jit(solution)/shard_map/ppermute | solution.py:16
  171.9 11.5 %collective-permute-start.3 = (f32[128,512]{1,0:T(8,128)S(1)}, f32[128,512]{1,0:T(8,128)S(1)}, u32[]{:S(2)}, u32[]{:S(2)}) collective-permute-start(f32[128,512]{1,0:T(8,128)S(1)} %add.43), channel_id=1, source_target_pairs={{0,256},{32,288},{64,320},{96,352},{128,384},{160,416},{192,448},{... | collective-permute-start | bytes 786440 | tf_op jit(solution)/shard_map/ppermute | solution.py:16
  183.4 21.9 %collective-permute-done.3 = f32[128,512]{1,0:T(8,128)S(1)} collective-permute-done((f32[128,512]{1,0:T(8,128)S(1)}, f32[128,512]{1,0:T(8,128)S(1)}, u32[]{:S(2)}, u32[]{:S(2)}) %collective-permute-start.3) | collective-permute-done | bytes 262176 | tf_op jit(solution)/shard_map/ppermute | solution.py:16
  205.4 0.0 copy-done.3
  205.4 1.3 constant_dynamic-update-slice_fusion.15
  206.7 0.0 copy-start
  206.9 22.9 %all_to_all.32 = f32[16,8,512]{2,1,0:T(8,128)S(1)} all-to-all(f32[16,8,512]{2,1,0:T(8,128)S(1)} %bitcast.62), channel_id=1, replica_groups=mesh['island'=16,'fsdp'=32] {'island'}, dimensions={0} | all-to-all | bytes 524288 | tf_op jit(solution)/shard_map/all_to_all | solution.py:47
  229.8 0.7 copy.31
  230.5 0.0 copy-done
  (18 shorter events, 0.2 us)
Async XLA Ops:
  7.2 102.2 %all-gather.3.cloned.1.call-start = ((), (), s32[]{:S(2)}) async-start(), calls=%async_computation.2 | async-start | bytes 12435456 | tf_op jit(solution)/shard_map/all_gather | solution.py:26
  11.7 97.6 %copy-start.1 = (f32[1,128,512]{2,1,0:T(8,128)S(1)}, f32[1,128,512]{2,1,0:T(8,128)}, u32[]{:S(2)}) copy-start(f32[1,128,512]{2,1,0:T(8,128)} %param.9) | copy-start | bytes 786436
  11.7 97.6 %copy-start.2 = (f32[1,128,512]{2,1,0:T(8,128)S(1)}, f32[1,128,512]{2,1,0:T(8,128)}, u32[]{:S(2)}) copy-start(f32[1,128,512]{2,1,0:T(8,128)} %param.10) | copy-start | bytes 786436
  109.4 96.0 %copy-start.3 = (f32[1,8,512]{2,1,0:T(8,128)S(1)}, f32[1,8,512]{2,1,0:T(8,128)}, u32[]{:S(2)}) copy-start(f32[1,8,512]{2,1,0:T(8,128)} %param.13) | copy-start | bytes 49156
  116.5 10.3 %collective-permute-start = (f32[128,512]{1,0:T(8,128)S(1)}, f32[128,512]{1,0:T(8,128)S(1)}, u32[]{:S(2)}, u32[]{:S(2)}) collective-permute-start(f32[128,512]{1,0:T(8,128)S(1)} %get-tuple-element.8), channel_id=1, source_target_pairs={{0,32},{32,0},{64,96},{96,64},{128,160},{160,128},{192,224},{224,1... | collective-permute-start | bytes 786440 | tf_op jit(solution)/shard_map/ppermute | solution.py:16
  126.9 16.1 %collective-permute-start.1 = (f32[128,512]{1,0:T(8,128)S(1)}, f32[128,512]{1,0:T(8,128)S(1)}, u32[]{:S(2)}, u32[]{:S(2)}) collective-permute-start(f32[128,512]{1,0:T(8,128)S(1)} %add.41), channel_id=1, source_target_pairs={{0,64},{32,96},{64,0},{96,32},{128,192},{160,224},{192,128},{224,1... | collective-permute-start | bytes 786440 | tf_op jit(solution)/shard_map/ppermute | solution.py:16
  143.0 28.9 %collective-permute-start.2 = (f32[128,512]{1,0:T(8,128)S(1)}, f32[128,512]{1,0:T(8,128)S(1)}, u32[]{:S(2)}, u32[]{:S(2)}) collective-permute-start(f32[128,512]{1,0:T(8,128)S(1)} %add.42), channel_id=1, source_target_pairs={{0,128},{32,160},{64,192},{96,224},{128,0},{160,32},{192,64},{224,... | collective-permute-start | bytes 786440 | tf_op jit(solution)/shard_map/ppermute | solution.py:16
  171.9 33.5 %collective-permute-start.3 = (f32[128,512]{1,0:T(8,128)S(1)}, f32[128,512]{1,0:T(8,128)S(1)}, u32[]{:S(2)}, u32[]{:S(2)}) collective-permute-start(f32[128,512]{1,0:T(8,128)S(1)} %add.43), channel_id=1, source_target_pairs={{0,256},{32,288},{64,320},{96,352},{128,384},{160,416},{192,448},{... | collective-permute-start | bytes 786440 | tf_op jit(solution)/shard_map/ppermute | solution.py:16
  206.7 23.8 %copy-start = (f32[8,512]{1,0:T(8,128)}, f32[8,512]{1,0:T(8,128)S(1)}, u32[]{:S(2)}) copy-start(f32[8,512]{1,0:T(8,128)S(1)} %get-tuple-element.6) | copy-start | bytes 49156
Sparse Core Ops, SparseCore 0:
  11.1 98.1 all-gather.2
